TPU v7x, 512 devices: a whole 4x8x8 slice. The times are simulated.
512 devices in a mesh: row: 32 (over z, y_lo), col: 4 (over y_hi, core), head: 4 (over x).
Axes of the slice: x: 4, y: 8 (y_hi: 2, y_lo: 4; y = y_hi * 4 + y_lo), z: 8, core: 2. Of those that a mesh axis runs over, the one named last changes fastest.
Arguments:
- tokens: bfloat16 [512, 128, 1024], P(('row', 'head'), 'col'), may hold values from -6 to 6
- valid: int32 [512, 128], P('row', 'col'), may hold values 0 or 1
- gain: float32 [1024], replicated, may hold values from 0.1 to 1.9
- w_qkv: bfloat16 [1024, 3, 1024], P(None, None, 'head'), may hold values from -0.1875 to 0.1875
- w_proj: bfloat16 [1024, 1024], P('head'), may hold values from -0.1875 to 0.1875
- rel_table: float32 [225, 16], P(None, 'head'), may hold values from -4 to 300
- cotangent: bfloat16 [512, 128, 1024], P(('row', 'head'), 'col'), may hold values from -24 to 24
Outputs:
- mixed: bfloat16 [512, 128, 1024], P(('row', 'head'), 'col')
- token_gradient: bfloat16 [512, 128, 1024], P(('row', 'head'), 'col')
- proj_grad: float32 [1024, 1024], P('head', ('row', 'col'))
- table_grad: float32 [225, 16], P(None, 'head')
All inputs are finite; a program needn't handle non-finite values. No bound on the sum of `valid` on one device may be relied on, other than what follows from the above.
Results may differ from a plain program's by a relative error of at most 0.0078.
Values may be sent and summed in bfloat16 or wider, within the bound.
No kernel may reach another device: no remote copies, remote signals or barrier semaphores. Data moves between devices by JAX's collectives and lax.ppermute only.
A program may use at most 64 MiB of HBM per device.

v0:
```python
import math
import jax
import jax.numpy as jnp
from jax import lax
from jax.sharding import PartitionSpec as P

HD = 64
WIN = 8
SHIFT = 4
EPS = 1e-05
HIGH = lax.Precision.HIGHEST


def passed_along(value, axis, steps):
    count = lax.axis_size(axis)
    pairs = [(source, (source + steps) % count) for source in range(count)]
    return lax.ppermute(value, axis, pairs)


def region(index, grand_total):
    return jnp.where(
        index < grand_total - WIN, 0, jnp.where(index < grand_total - SHIFT, 1, 2)
    ).astype(jnp.int32)


def offsets():
    span = 2 * WIN - 1
    pos = jnp.arange(WIN * WIN, dtype=jnp.int32)
    prow = pos // WIN
    pcol = pos % WIN
    index = (prow[:, None] - prow[None, :] + WIN - 1) * span + (
        pcol[:, None] - pcol[None, :] + WIN - 1
    )
    table_ids = jnp.arange(span * span, dtype=jnp.int32)
    return (
        (index[:, :, None] == table_ids[None, None, :])
        .astype(jnp.float32)
        .reshape(WIN * WIN * WIN * WIN, span * span)
    )


def to_windows(block):
    nrow, ncol, heads, depth = block.shape
    block = block.reshape(nrow // WIN, WIN, ncol // WIN, WIN, heads, depth).transpose(
        0, 2, 4, 1, 3, 5
    )
    return block.reshape(nrow // WIN * (ncol // WIN), heads, WIN * WIN, depth)


def from_windows(block, nrow, ncol):
    count, heads, posn, depth = block.shape
    block = block.reshape(nrow // WIN, ncol // WIN, heads, WIN, WIN, depth).transpose(
        0, 3, 1, 4, 2, 5
    )
    return block.reshape(nrow, ncol, heads * depth)


def rows_in(block):
    return jnp.concatenate([block[SHIFT:], passed_along(block[:SHIFT], "row", -1)], 0)


def cols_in(block):
    return jnp.concatenate([block[:, SHIFT:], passed_along(block[:, :SHIFT], "col", -1)], 1)


def rows_out(block):
    return jnp.concatenate([passed_along(block[-SHIFT:], "row", 1), block[:-SHIFT]], 0)


def cols_out(block):
    return jnp.concatenate([passed_along(block[:, -SHIFT:], "col", 1), block[:, :-SHIFT]], 1)


def roll_in(block):
    return cols_in(rows_in(block))


def roll_out(block):
    return cols_out(rows_out(block))


def roll_pair(first, second, roller):
    return (roller(first), roller(second))


def head_sum(term_fn, part_rows):
    return lax.psum_scatter(
        term_fn(jnp.int32(0), lax.axis_size("head") * part_rows).astype(jnp.bfloat16),
        "head",
        scatter_dimension=0,
        tiled=True,
    ).astype(jnp.float32)


def attend(qkv, grad, labels, valid, bias, onehot):
    nrow, ncol = labels.shape
    feature_width = qkv.shape[3]
    heads = feature_width // HD
    scale = HD ** (-0.5)
    f32 = jnp.float32
    query = to_windows(qkv[:, :, 0].reshape(nrow, ncol, heads, HD))
    key = to_windows(qkv[:, :, 1].reshape(nrow, ncol, heads, HD))
    value = to_windows(qkv[:, :, 2].reshape(nrow, ncol, heads, HD))
    dout = to_windows(grad.reshape(nrow, ncol, heads, HD))
    lab_win = to_windows(labels[:, :, None, None])[:, 0, :, 0]
    val_win = to_windows(valid[:, :, None, None])[:, 0, :, 0]
    diagonal = jnp.eye(WIN * WIN, dtype=bool)
    allowed = (lab_win[:, :, None] == lab_win[:, None, :]) & (
        (val_win[:, None, :] == 1) | diagonal[None]
    )
    scores = (
        jnp.einsum("wiqd,wikd->wiqk", query, key, preferred_element_type=f32) * scale + bias[None]
    )
    scores = jnp.where(allowed[:, None], scores, -1e30)
    top = jnp.max(scores, -1, keepdims=True)
    expo = jnp.exp(scores - top)
    prob = expo / jnp.sum(expo, -1, keepdims=True)
    prob_b = prob.astype(jnp.bfloat16)
    attended = jnp.einsum("wiqk,wikd->wiqd", prob_b, value, preferred_element_type=f32).astype(
        jnp.bfloat16
    )
    dprob = jnp.einsum("wiqd,wikd->wiqk", dout, value, preferred_element_type=f32)
    dvalue = jnp.einsum("wiqk,wiqd->wikd", prob_b, dout, preferred_element_type=f32).astype(
        jnp.bfloat16
    )
    dscore = prob * (dprob - jnp.sum(prob * dprob, -1, keepdims=True))
    dscore_b = dscore.astype(jnp.bfloat16)
    dquery = (
        jnp.einsum("wiqk,wikd->wiqd", dscore_b, key, preferred_element_type=f32) * scale
    ).astype(jnp.bfloat16)
    dkey = (
        jnp.einsum("wiqk,wiqd->wikd", dscore_b, query, preferred_element_type=f32) * scale
    ).astype(jnp.bfloat16)
    summed = jnp.sum(dscore, 0).transpose(1, 2, 0).reshape(WIN * WIN * WIN * WIN, heads)
    tgrad = jnp.dot(onehot.T, summed, precision=HIGH)
    grads = jnp.stack(
        [
            from_windows(dquery, nrow, ncol),
            from_windows(dkey, nrow, ncol),
            from_windows(dvalue, nrow, ncol),
        ],
        2,
    )
    return (from_windows(attended, nrow, ncol), grads, tgrad)


def on_device(tokens, valid, gain, w_qkv, w_proj, rel_table, cotangent):
    part_rows, ncol, feature_width = tokens.shape
    tile_rows = part_rows * lax.axis_size("head")
    row_count = lax.axis_size("row")
    col_count = lax.axis_size("col")
    flat = tokens.astype(jnp.float32)
    token_average = jnp.mean(flat, -1, keepdims=True)
    centered_input = flat - token_average
    inverse_deviation = lax.rsqrt(
        jnp.mean(centered_input * centered_input, -1, keepdims=True) + EPS
    )
    standardized_input = centered_input * inverse_deviation
    normalized_tokens = (standardized_input * gain).astype(jnp.bfloat16)
    grad_tile = lax.all_gather(cotangent, "head", axis=0, tiled=True)
    out_grad = jnp.einsum(
        "rcd,nd->rcn", grad_tile, w_proj, preferred_element_type=jnp.float32
    ).astype(jnp.bfloat16)
    source = lax.all_gather(normalized_tokens, "head", axis=0, tiled=True)
    moved, rolled_grad = roll_pair(source, out_grad, roll_in)
    rolled = jnp.einsum("rcd,dtn->rctn", moved, w_qkv, preferred_element_type=jnp.float32).astype(
        jnp.bfloat16
    )
    row_lab = region(
        lax.axis_index("row") * tile_rows + jnp.arange(tile_rows, dtype=jnp.int32),
        tile_rows * row_count,
    )
    col_lab = region(
        lax.axis_index("col") * ncol + jnp.arange(ncol, dtype=jnp.int32), ncol * col_count
    )
    labels = 3 * row_lab[:, None] + col_lab[None, :]
    onehot = offsets()
    heads = rel_table.shape[1]
    bias = (
        jnp.dot(onehot, rel_table, precision=HIGH)
        .reshape(WIN * WIN, WIN * WIN, heads)
        .transpose(2, 0, 1)
    )
    attended, grads, tgrad = attend(rolled, rolled_grad, labels, valid, bias, onehot)
    attn_out, qkv_grad = roll_pair(attended, grads, roll_out)

    def proj_term(start, count):
        return jnp.einsum("rcn,nd->rcd", attn_out, w_proj, preferred_element_type=jnp.float32)

    def back_term(start, count):
        return jnp.einsum("rctn,dtn->rcd", qkv_grad, w_qkv, preferred_element_type=jnp.float32)

    mixed = (flat + head_sum(proj_term, part_rows)).astype(jnp.bfloat16)
    norm_grad = head_sum(back_term, part_rows)
    scale = 1.0 / math.sqrt(tile_rows * ncol * row_count * col_count)
    weight_term = jnp.einsum("rcn,rcd->nd", attn_out, grad_tile, preferred_element_type=jnp.float32)
    proj_grad = (
        lax.psum_scatter(weight_term, ("row", "col"), scatter_dimension=1, tiled=True) * scale
    )
    table_grad = lax.psum(tgrad, ("row", "col")) * (WIN * scale)
    scaled_tokens = norm_grad * gain
    token_gradient = cotangent.astype(jnp.float32) + inverse_deviation * (
        scaled_tokens
        - jnp.mean(scaled_tokens, -1, keepdims=True)
        - standardized_input * jnp.mean(scaled_tokens * standardized_input, -1, keepdims=True)
    )
    return (mixed, token_gradient.astype(jnp.bfloat16), proj_grad, table_grad)


def solution(mesh):
    return jax.shard_map(
        on_device,
        mesh=mesh,
        in_specs=(
            P(("row", "head"), "col", None),
            P("row", "col"),
            P(),
            P(None, None, "head"),
            P("head", None),
            P(None, "head"),
            P(("row", "head"), "col", None),
        ),
        out_specs=(
            P(("row", "head"), "col", None),
            P(("row", "head"), "col", None),
            P("head", ("row", "col")),
            P(None, "head"),
        ),
        check_vma=False,
    )
```

profile of v0, /device:TPU:8, one launch (start us, length us, event | category | flops | bytes accessed | tf_op | source)
XLA Modules:
  0.0 753.7 jit_solution(1386446947580851297)
XLA Ops:
  7.2 1.2 convert_reduce_fusion
  8.5 1.2 fusion.36
  10.2 1.9 fusion.30
  14.0 3.4 fusion.17
  17.5 28.7 %all-gather.3.cloned.1.call-done = bf16[16,32,1024]{2,1,0:T(8,128)(2,1)} async-done(((bf16[4,32,1024]{2,1,0:T(8,128)(2,1)}), bf16[16,32,1024]{2,1,0:T(8,128)(2,1)}) %all-gather.3.cloned.1.call-update) | async-done | bytes 1048592 | tf_op jit(solution)/shard_map/all_gather | solution.py:164
  46.2 1.8 slice.77
  47.9 2.4 collective-permute-start
  50.4 27.6 %all-gather.5.cloned.1.call-done = bf16[16,32,1024]{2,1,0:T(8,128)(2,1)} async-done(((bf16[4,32,1024]{2,1,0:T(8,128)(2,1)}), bf16[16,32,1024]{2,1,0:T(8,128)(2,1)}) %all-gather.5.cloned.1.call-update) | async-done | bytes 1048592 | tf_op jit(solution)/shard_map/all_gather | solution.py:160
  78.0 1.7 convolution_convert_fusion.3
  79.7 2.4 collective-permute-start.4
  84.4 1.4 collective-permute-done.4
  86.5 4.2 collective-permute-start.5
  91.5 4.3 collective-permute-start.1
  96.1 2.2 collective-permute-done.1
  98.3 1.0 fusion.9
  100.5 1.2 reshape_reshape_squeeze.10
  103.3 1.2 fusion.57
  104.5 1.2 reshape_reshape_squeeze.11
  106.7 3.0 convolution_convert_fusion.2
  109.7 1.7 copy.46
  111.4 1.0 reshape.236
  113.3 2.5 collective-permute-start.2
  115.8 1.7 pad_maximum_fusion.2
  117.5 1.2 reshape_reshape.3
  120.9 4.4 collective-permute-start.3
  125.4 2.9 convolution_convert_fusion.1
  128.3 1.7 copy.55
  130.0 1.0 stack_reshape.11
  131.1 2.8 convolution_bitcast_fusion
  134.2 1.9 multiply_reduce_fusion
  136.4 1.2 fusion.16
  137.6 1.3 copy.53
  138.9 1.5 copy.54
  140.4 2.2 stack_reshape.10
  144.4 6.4 collective-permute-start.6
  150.8 7.1 collective-permute-done.6
  157.9 2.4 collective-permute-start.7
  160.3 7.9 %collective-permute-done.7 = bf16[16,4,3,256]{3,1,2,0:T(4,128)(2,1)S(1)} collective-permute-done((bf16[16,4,3,256]{3,1,2,0:T(4,128)(2,1)S(1)}, bf16[16,4,3,256]{3,1,2,0:T(4,128)(2,1)S(1)}, u32[]{:S(2)}, u32[]{:S(2)}) %collective-permute-start.7) | collective-permute-done | bytes 98336 | tf_op jit(solution)/shard_map/ppermute | solution.py:17
  168.2 2.0 bitcast_convert_fusion
  170.3 1.5 convolution_convert_fusion
  172.0 1.4 fusion.18
  173.4 266.7 %psum.7 = f32[225,4]{0,1:T(4,128)S(1)} all-reduce(f32[225,4]{0,1:T(4,128)S(1)} %fusion.18), channel_id=1, replica_groups=mesh['row'=32,'col'=4,'head'=4] {'row','col'}, use_global_device_ids=true, to_apply=%region_11.12 | all-reduce | flops 900 | bytes 7200 | tf_op jit(solution)/shard_map/psum | solution.py:200
  440.7 237.8 %reduce-scatter.8.cloned.1.call-done = f32[256,8]{0,1:T(8,128)} async-done(((f32[256,1024]{0,1:T(8,128)}), f32[256,8]{0,1:T(8,128)}) %reduce-scatter.8.cloned.1.call-update) | async-done | bytes 8208 | tf_op jit(solution)/shard_map/reduce_scatter | solution.py:198
  678.5 1.3 broadcast_multiply_fusion
  679.8 34.0 %reduce-scatter.6.cloned.1.call-done = bf16[4,32,1024]{2,1,0:T(8,128)(2,1)} async-done(((bf16[16,32,1024]{2,1,0:T(8,128)(2,1)}), bf16[4,32,1024]{2,1,0:T(8,128)(2,1)}) %reduce-scatter.6.cloned.1.call-update) | async-done | bytes 262160 | tf_op jit(solution)/shard_map/reduce_scatter | solution.py:87
  713.8 1.2 fusion.40
  715.0 30.1 %reduce-scatter.4.cloned.1.call-done = bf16[4,32,1024]{2,1,0:T(8,128)(2,1)} async-done(((bf16[16,32,1024]{2,1,0:T(8,128)(2,1)}), bf16[4,32,1024]{2,1,0:T(8,128)(2,1)}) %reduce-scatter.4.cloned.1.call-update) | async-done | bytes 262160 | tf_op jit(solution)/shard_map/reduce_scatter | solution.py:87
  745.1 2.1 fusion.35
  (107 shorter events, 16.3 us)
Async XLA Ops:
  7.2 91.1 %copy-start = (bf16[1024,3,256]{2,0,1:T(8,128)(2,1)S(1)}, bf16[1024,3,256]{2,0,1:T(8,128)(2,1)}, u32[]{:S(2)}) copy-start(bf16[1024,3,256]{2,0,1:T(8,128)(2,1)} %param.10) | copy-start | bytes 4718596
  7.2 5.9 copy-start.21
  7.2 6.8 copy-start.22
  7.2 38.9 %all-gather.3.cloned.1.call-start = ((), (), s32[]{:S(2)}) async-start(), calls=%async_computation.3 | async-start | bytes 1310720 | tf_op jit(solution)/shard_map/all_gather | solution.py:164
  8.4 1.3 copy-start.14
  8.4 69.5 %copy-start.8 = (bf16[256,1024]{1,0:T(8,128)(2,1)S(1)}, bf16[256,1024]{1,0:T(8,128)(2,1)}, u32[]{:S(2)}) copy-start(bf16[256,1024]{1,0:T(8,128)(2,1)} %param.11) | copy-start | bytes 1572868
  9.7 0.5 copy-start.17
  12.1 65.8 %all-gather.5.cloned.1.call-start = ((), (), s32[]{:S(2)}) async-start(), calls=%async_computation.5 | async-start | bytes 1310720 | tf_op jit(solution)/shard_map/all_gather | solution.py:160
  12.9 665.6 %reduce-scatter.8.cloned.1.call-start = ((), (), s32[]{:S(2)}) async-start(), calls=%async_computation.7 | async-start | bytes 1056768 | tf_op jit(solution)/shard_map/reduce_scatter | solution.py:198
  13.4 0.6 copy-start.19
  46.1 38.2 %copy-start.6 = (bf16[16,32,1024]{2,1,0:T(8,128)(2,1)S(1)}, bf16[16,32,1024]{2,1,0:T(8,128)(2,1)}, u32[]{:S(2)}) copy-start(bf16[16,32,1024]{2,1,0:T(8,128)(2,1)} %all-gather.3.cloned.1.call-done) | copy-start | bytes 3145732
  47.9 43.5 %collective-permute-start = (bf16[4,32,1024]{2,1,0:T(8,128)(2,1)}, bf16[4,32,1024]{2,1,0:T(8,128)(2,1)S(1)}, u32[]{:S(2)}, u32[]{:S(2)}) collective-permute-start(bf16[4,32,1024]{2,1,0:T(8,128)(2,1)} %slice.77), channel_id=1, source_target_pairs={{0,496},{16,0},{32,16},{48,32},{64,48},{80,64},{96,80},{112,96},{1... | collective-permute-start | bytes 786440 | tf_op jit(solution)/shard_map/ppermute | solution.py:17
  79.7 2.5 copy-start.11
  79.7 6.2 collective-permute-start.4
  86.5 29.3 %collective-permute-start.5 = (bf16[16,4,256]{2,1,0:T(4,128)(2,1)}, bf16[16,4,256]{2,1,0:T(4,128)(2,1)}, u32[]{:S(2)}, u32[]{:S(2)}) collective-permute-start(bf16[16,4,256]{2,1,0:T(4,128)(2,1)} %pad_maximum_fusion.5), channel_id=1, source_target_pairs={{0,12},{4,0},{8,4},{12,8},{1,13},{5,1},{9,5},{13,9},{2,14},{6,2},{... | collective-permute-start | bytes 98312 | tf_op jit(solution)/shard_map/ppermute | solution.py:17
  91.5 6.8 collective-permute-start.1
  102.3 1.0 copy-start.3
  113.3 7.6 %collective-permute-start.2 = (bf16[4,32,256]{2,1,0:T(8,128)(2,1)S(1)}, bf16[4,32,256]{2,1,0:T(8,128)(2,1)S(1)}, u32[]{:S(2)}, u32[]{:S(2)}) collective-permute-start(bf16[4,32,256]{2,1,0:T(8,128)(2,1)S(1)} %slice.83), channel_id=1, source_target_pairs={{0,16},{16,32},{32,48},{48,64},{64,80},{80,96},{96,112},{112,128},... | collective-permute-start | bytes 196616 | tf_op jit(solution)/shard_map/ppermute | solution.py:17
  120.9 10.1 %collective-permute-start.3 = (bf16[16,4,256]{2,1,0:T(4,128)(2,1)S(1)}, bf16[16,4,256]{2,1,0:T(4,128)(2,1)S(1)}, u32[]{:S(2)}, u32[]{:S(2)}) collective-permute-start(bf16[16,4,256]{2,1,0:T(4,128)(2,1)S(1)} %pad_maximum_fusion.6), channel_id=1, source_target_pairs={{0,4},{4,8},{8,12},{12,0},{1,5},{5,9},{9,13},{13,1},{2,6},{6,10},{... | collective-permute-start | bytes 98312 | tf_op jit(solution)/shard_map/ppermute | solution.py:17
  131.1 3.1 copy-start.10
  131.1 2.8 copy-start.12
  133.9 579.8 %reduce-scatter.6.cloned.1.call-start = ((), (), s32[]{:S(2)}) async-start(), calls=%async_computation.6 | async-start | bytes 1310720 | tf_op jit(solution)/shard_map/reduce_scatter | solution.py:87
  134.2 1.9 copy-start.2
  142.9 1.4 copy-start.5
  143.2 1.1 copy-start.4
  144.4 13.5 %collective-permute-start.6 = (bf16[4,32,3,256]{3,1,2,0:T(8,128)(2,1)S(1)}, bf16[4,32,3,256]{3,1,2,0:T(8,128)(2,1)S(1)}, u32[]{:S(2)}, u32[]{:S(2)}) collective-permute-start(bf16[4,32,3,256]{3,1,2,0:T(8,128)(2,1)S(1)} %slice.89), channel_id=1, source_target_pairs={{0,16},{16,32},{32,48},{48,64},{64,80},{80,96},{96,112},{112,128},... | collective-permute-start | bytes 589832 | tf_op jit(solution)/shard_map/ppermute | solution.py:17
  157.9 12.4 %copy-start.9 = (bf16[256,1024]{1,0:T(8,128)(2,1)S(1)}, bf16[256,1024]{1,0:T(8,128)(2,1)}, u32[]{:S(2)}) copy-start(bf16[256,1024]{1,0:T(8,128)(2,1)} %param.11) | copy-start | bytes 1572868
  157.9 12.4 %copy-start.13 = (bf16[16,4,256]{2,1,0:T(4,128)(2,1)S(1)}, bf16[16,4,256]{2,1,0:T(4,128)(2,1)}, u32[]{:S(2)}) copy-start(bf16[16,4,256]{2,1,0:T(4,128)(2,1)} %copy-done.12) | copy-start | bytes 98308
  157.9 10.3 %collective-permute-start.7 = (bf16[16,4,3,256]{3,1,2,0:T(4,128)(2,1)S(1)}, bf16[16,4,3,256]{3,1,2,0:T(4,128)(2,1)S(1)}, u32[]{:S(2)}, u32[]{:S(2)}) collective-permute-start(bf16[16,4,3,256]{3,1,2,0:T(4,128)(2,1)S(1)} %pad_maximum_fusion.4), channel_id=1, source_target_pairs={{0,4},{4,8},{8,12},{12,0},{1,5},{5,9},{9,13},{13,1},{2,6},{6,10},{... | collective-permute-start | bytes 294920 | tf_op jit(solution)/shard_map/ppermute | solution.py:17
  170.3 1.7 copy-start.20
  170.3 574.9 %reduce-scatter.4.cloned.1.call-start = ((), (), s32[]{:S(2)}) async-start(), calls=%async_computation.4 | async-start | bytes 1310720 | tf_op jit(solution)/shard_map/reduce_scatter | solution.py:87
  171.8 542.0 %copy-start.1 = (bf16[4,32,1024]{2,1,0:T(8,128)(2,1)S(1)}, bf16[4,32,1024]{2,1,0:T(8,128)(2,1)}, u32[]{:S(2)}) copy-start(bf16[4,32,1024]{2,1,0:T(8,128)(2,1)} %param.7) | copy-start | bytes 786436
  171.8 542.0 %copy-start.15 = (f32[4,32]{1,0:T(4,128)S(1)}, f32[4,32]{1,0:T(4,128)}, u32[]{:S(2)}) copy-start(f32[4,32]{1,0:T(4,128)} %copy-done.14) | copy-start | bytes 1540
  171.8 542.0 %copy-start.16 = (f32[1024]{0:T(1024)S(1)}, f32[1024]{0:T(1024)}, u32[]{:S(2)}) copy-start(f32[1024]{0:T(1024)} %param.9) | copy-start | bytes 12292
  171.8 542.0 %copy-start.18 = (f32[4,32]{1,0:T(4,128)S(1)}, f32[4,32]{1,0:T(4,128)}, u32[]{:S(2)}) copy-start(f32[4,32]{1,0:T(4,128)} %copy-done.17) | copy-start | bytes 1540
  171.8 573.3 %copy-start.7 = (bf16[4,32,1024]{2,1,0:T(8,128)(2,1)S(1)}, bf16[4,32,1024]{2,1,0:T(8,128)(2,1)}, u32[]{:S(2)}) copy-start(bf16[4,32,1024]{2,1,0:T(8,128)(2,1)} %param.13) | copy-start | bytes 786436
Sparse Core Ops, SparseCore 0:
  12.3 33.8 all-gather.2
  48.2 29.6 all-gather.4
  134.0 544.4 reduce-scatter.7
  681.4 32.2 reduce-scatter.5
  716.4 28.6 reduce-scatter.3
where the time goes:
time: 755 us; the launch traced here: 754 us
  waiting for transfers between devices  378 us (50%)
  blocking collectives  267 us (35%)
  starting transfers between devices  29.4 us (4%)
  local copies, waits for them, and re-layouts  26.9 us (4%)
  matrix products  23.6 us (3%)
  other arithmetic  14.9 us (2%)
  between operations  14.4 us (2%)
    psum x1, blocking collectives, on_device(): table_grad = lax.psum(tgrad, ('row', 'col')) * (WIN * scale)  267 us
    reduce_scatter x1, waiting for transfers between devices, on_device(): lax.psum_scatter(weight_term, ('row', 'col'), scatter_dimension=1, tiled=...  238 us
    reduce_scatter x2, waiting for transfers between devices, head_sum(): lax.psum_scatter(term_fn(jnp.int32(0), lax.axis_size('head') * part_rows)...  64.1 us
    ppermute x8, starting transfers between devices, passed_along(): return lax.ppermute(value, axis, pairs)  29 us
    all_gather x1, waiting for transfers between devices, on_device(): source = lax.all_gather(normalized_tokens, 'head', axis=0, tiled=True)  28.7 us
    all_gather x1, waiting for transfers between devices, on_device(): grad_tile = lax.all_gather(cotangent, 'head', axis=0, tiled=True)  27.6 us
    ppermute x8, waiting for transfers between devices, passed_along(): return lax.ppermute(value, axis, pairs)  19 us
  transfers between devices with their start and end apart: 13, of which 10 were waited for; matrix products, arithmetic and copies ran while one was open for 7% of the time, Pallas kernels for 0%

commit v1 on v0

--- a/solution.py
+++ b/solution.py
@@ -3,12 +3,21 @@
 import jax.numpy as jnp
 from jax import lax
 from jax.sharding import PartitionSpec as P
+from jax.lax import axis_index, axis_size, ppermute
 
 HD = 64
 WIN = 8
 SHIFT = 4
 EPS = 1e-05
 HIGH = lax.Precision.HIGHEST
+
+
+def _fix_vector(q_in, join_dim):
+    q_in = jnp.moveaxis(q_in, 0, join_dim)
+    arr_now = q_in.shape
+    return q_in.reshape(
+        *arr_now[:join_dim], arr_now[join_dim] * arr_now[join_dim + 1], *arr_now[join_dim + 2 :]
+    )
 
 
 def passed_along(value, axis, steps):
@@ -157,7 +166,23 @@
     )
     standardized_input = centered_input * inverse_deviation
     normalized_tokens = (standardized_input * gain).astype(jnp.bfloat16)
-    grad_tile = lax.all_gather(cotangent, "head", axis=0, tiled=True)
+
+    def regions_meet(state, which_axis, k_dim):
+        p_count = axis_size(which_axis)
+        heap = [(t, (t + 1) % p_count) for t in range(p_count)]
+        block_list = [(k0, c) for c, k0 in heap]
+        high, b_now = ([], [])
+        for dd in [*range(p_count - 1)]:
+            if dd % 2 == 0:
+                high.append(ppermute(high[-1] if high else state, which_axis, heap))
+            else:
+                b_now.append(ppermute(b_now[-1] if b_now else state, which_axis, block_list))
+        finding = jnp.stack([*high[::-1], state, *b_now])
+        u1 = axis_index(which_axis) - len(high)
+        finding = finding[(jnp.arange(p_count) - u1) % p_count]
+        return _fix_vector(finding, k_dim)
+
+    grad_tile = regions_meet(cotangent, "head", 0)
     out_grad = jnp.einsum(
         "rcd,nd->rcn", grad_tile, w_proj, preferred_element_type=jnp.float32
     ).astype(jnp.bfloat16)

time: 755 us -> 726 us (0.962)
  waiting for transfers between devices: 378 us -> 336 us
  starting transfers between devices: 29.4 us -> 39.1 us
    all_gather x1 -> x0, waiting for transfers between devices: 27.6 us -> none  [on_device(): grad_tile = lax.all_gather(cotangent, 'head', axis=0, tiled=True)]
    all_gather x1, waiting for transfers between devices: 28.7 us -> 10.5 us  [on_device(): source = lax.all_gather(normalized_tokens, 'head', axis=0, tiled=True)]
    ppermute x0 -> x3, starting transfers between devices: none -> 9.37 us  [the longest x2 5.71 us: regions_meet(): high.append(ppermute(high[-1] if high else state, which_axis, heap))]
  transfers between devices with their start and end apart: 13 -> 15, of which waited for: 10 -> 9; matrix products, arithmetic and copies ran while one was open for 7% -> 8% of each run, Pallas kernels for 0% -> 0%
where the time goes in v1:
time: 726 us; the launch traced here: 725 us
  waiting for transfers between devices  336 us (46%)
  blocking collectives  267 us (37%)
  starting transfers between devices  39.1 us (5%)
  local copies, waits for them, and re-layouts  24.5 us (3%)
  matrix products  23.9 us (3%)
  other arithmetic  19.5 us (3%)
  between operations  14.4 us (2%)
    psum x1, blocking collectives, on_device(): table_grad = lax.psum(tgrad, ('row', 'col')) * (WIN * scale)  267 us
    reduce_scatter x1, waiting for transfers between devices, on_device(): lax.psum_scatter(weight_term, ('row', 'col'), scatter_dimension=1, tiled=...  236 us
    reduce_scatter x2, waiting for transfers between devices, head_sum(): lax.psum_scatter(term_fn(jnp.int32(0), lax.axis_size('head') * part_rows)...  63.6 us
    ppermute x8, starting transfers between devices, passed_along(): return lax.ppermute(value, axis, pairs)  29.4 us
    ppermute x8, waiting for transfers between devices, passed_along(): return lax.ppermute(value, axis, pairs)  22.1 us
  transfers between devices with their start and end apart: 15, of which 9 were waited for; matrix products, arithmetic and copies ran while one was open for 8% of the time, Pallas kernels for 0%

profile of v1, /device:TPU:8, one launch (start us, length us, event | category | flops | bytes accessed | tf_op | source)
XLA Modules:
  0.0 725.1 jit_solution(6384101965422095429)
XLA Ops:
  7.2 3.5 collective-permute-start.4
  10.8 3.7 collective-permute-start.6
  15.5 1.2 fusion.36
  17.3 1.9 fusion.30
  20.2 2.2 collective-permute-start.5
  22.7 4.1 fusion.17
  26.8 4.0 collective-permute-done.5
  30.8 1.1 pad_maximum_fusion
  31.9 1.9 gather_fusion
  35.0 6.6 collective-permute-start.7
  41.6 10.5 %all-gather.2.cloned.1.call-done = bf16[16,32,1024]{2,1,0:T(8,128)(2,1)} async-done(((bf16[4,32,1024]{2,1,0:T(8,128)(2,1)}), bf16[16,32,1024]{2,1,0:T(8,128)(2,1)}) %all-gather.2.cloned.1.call-update) | async-done | bytes 1048592 | tf_op jit(solution)/shard_map/all_gather | solution.py:189
  53.0 2.4 collective-permute-start
  57.4 1.4 pad_maximum_fusion.6
  58.8 5.6 collective-permute-start.8
  64.4 1.6 slice_maximum_fusion.1
  66.2 3.8 collective-permute-start.1
  70.2 2.3 collective-permute-done.1
  74.7 1.2 reshape_reshape_squeeze.10
  76.0 1.2 fusion.14
  78.3 1.3 fusion.59
  80.7 2.9 convolution_convert_fusion.2
  83.7 1.7 copy.46
  85.8 2.4 collective-permute-start.2
  88.2 1.7 pad_maximum_fusion.3
  89.9 1.2 reshape_reshape.3
  93.9 4.5 collective-permute-start.3
  98.3 2.9 convolution_convert_fusion.1
  101.3 1.7 copy.55
  104.0 2.8 convolution_bitcast_fusion
  107.1 1.9 multiply_reduce_fusion
  110.0 1.2 fusion.16
  111.2 1.3 copy.53
  112.6 1.5 copy.54
  114.0 2.2 stack_reshape.10
  118.0 1.9 collective-permute-start.9
  120.0 11.1 %collective-permute-done.9 = bf16[4,32,3,256]{3,1,2,0:T(8,128)(2,1)S(1)} collective-permute-done((bf16[4,32,3,256]{3,1,2,0:T(8,128)(2,1)S(1)}, bf16[4,32,3,256]{3,1,2,0:T(8,128)(2,1)S(1)}, u32[]{:S(2)}, u32[]{:S(2)}) %collective-permute-start.9) | collective-permute-done | bytes 196640 | tf_op jit(solution)/shard_map/ppermute | solution.py:26
  131.1 2.2 collective-permute-start.10
  133.3 7.8 %collective-permute-done.10 = bf16[16,4,3,256]{3,1,2,0:T(4,128)(2,1)S(1)} collective-permute-done((bf16[16,4,3,256]{3,1,2,0:T(4,128)(2,1)S(1)}, bf16[16,4,3,256]{3,1,2,0:T(4,128)(2,1)S(1)}, u32[]{:S(2)}, u32[]{:S(2)}) %collective-permute-start.10) | collective-permute-done | bytes 98336 | tf_op jit(solution)/shard_map/ppermute | solution.py:26
  141.1 2.1 bitcast_convert_fusion
  143.3 1.4 convolution_convert_fusion
  144.9 1.4 fusion.18
  146.3 267.5 %psum.7 = f32[225,4]{0,1:T(4,128)S(1)} all-reduce(f32[225,4]{0,1:T(4,128)S(1)} %fusion.18), channel_id=1, replica_groups=mesh['row'=32,'col'=4,'head'=4] {'row','col'}, use_global_device_ids=true, to_apply=%region_11.12 | all-reduce | flops 900 | bytes 7200 | tf_op jit(solution)/shard_map/psum | solution.py:225
  414.4 236.0 %reduce-scatter.8.cloned.1.call-done = f32[256,8]{0,1:T(8,128)} async-done(((f32[256,1024]{0,1:T(8,128)}), f32[256,8]{0,1:T(8,128)}) %reduce-scatter.8.cloned.1.call-update) | async-done | bytes 8208 | tf_op jit(solution)/shard_map/reduce_scatter | solution.py:223
  650.3 1.3 broadcast_multiply_fusion
  651.6 33.4 %reduce-scatter.6.cloned.1.call-done = bf16[4,32,1024]{2,1,0:T(8,128)(2,1)} async-done(((bf16[16,32,1024]{2,1,0:T(8,128)(2,1)}), bf16[4,32,1024]{2,1,0:T(8,128)(2,1)}) %reduce-scatter.6.cloned.1.call-update) | async-done | bytes 262160 | tf_op jit(solution)/shard_map/reduce_scatter | solution.py:96
  685.1 1.2 fusion.40
  686.3 30.2 %reduce-scatter.4.cloned.1.call-done = bf16[4,32,1024]{2,1,0:T(8,128)(2,1)} async-done(((bf16[16,32,1024]{2,1,0:T(8,128)(2,1)}), bf16[4,32,1024]{2,1,0:T(8,128)(2,1)}) %reduce-scatter.4.cloned.1.call-update) | async-done | bytes 262160 | tf_op jit(solution)/shard_map/reduce_scatter | solution.py:96
  716.5 2.1 fusion.35
  (112 shorter events, 19.6 us)
Async XLA Ops:
  7.2 65.4 %copy-start = (bf16[1024,3,256]{2,0,1:T(8,128)(2,1)S(1)}, bf16[1024,3,256]{2,0,1:T(8,128)(2,1)}, u32[]{:S(2)}) copy-start(bf16[1024,3,256]{2,0,1:T(8,128)(2,1)} %param.10) | copy-start | bytes 4718596
  7.2 23.6 %copy-start.9 = (bf16[4,32,1024]{2,1,0:T(8,128)(2,1)S(1)}, bf16[4,32,1024]{2,1,0:T(8,128)(2,1)}, u32[]{:S(2)}) copy-start(bf16[4,32,1024]{2,1,0:T(8,128)(2,1)} %param.13) | copy-start | bytes 786436
  7.2 44.9 %all-gather.2.cloned.1.call-start = ((), (), s32[]{:S(2)}) async-start(), calls=%async_computation.3 | async-start | bytes 1310720 | tf_op jit(solution)/shard_map/all_gather | solution.py:189
  7.2 13.0 %collective-permute-start.4 = (bf16[4,32,1024]{2,1,0:T(8,128)(2,1)}, bf16[4,32,1024]{2,1,0:T(8,128)(2,1)S(1)}, u32[]{:S(2)}, u32[]{:S(2)}) collective-permute-start(bf16[4,32,1024]{2,1,0:T(8,128)(2,1)} %param.13), channel_id=1, source_target_pairs={{0,1},{1,2},{2,3},{3,0},{4,5},{5,6},{6,7},{7,4},{8,9},{9,10},{10,1... | collective-permute-start | bytes 786440 | tf_op jit(solution)/shard_map/ppermute | solution.py:177
  10.8 16.1 %collective-permute-start.6 = (bf16[4,32,1024]{2,1,0:T(8,128)(2,1)}, bf16[4,32,1024]{2,1,0:T(8,128)(2,1)S(1)}, u32[]{:S(2)}, u32[]{:S(2)}) collective-permute-start(bf16[4,32,1024]{2,1,0:T(8,128)(2,1)} %param.13), channel_id=1, source_target_pairs={{1,0},{2,1},{3,2},{0,3},{5,4},{6,5},{7,6},{4,7},{9,8},{10,9},{11,1... | collective-permute-start | bytes 786440 | tf_op jit(solution)/shard_map/ppermute | solution.py:179
  15.5 1.2 copy-start.15
  16.7 0.6 copy-start.18
  19.2 631.1 %reduce-scatter.8.cloned.1.call-start = ((), (), s32[]{:S(2)}) async-start(), calls=%async_computation.6 | async-start | bytes 1056768 | tf_op jit(solution)/shard_map/reduce_scatter | solution.py:223
  20.1 10.7 %copy-start.20 = (s32[64,64]{1,0:T(8,128)}, s32[64,64]{1,0:T(8,128)S(1)}, u32[]{:S(2)}) copy-start(s32[64,64]{1,0:T(8,128)S(1)} %add_add_fusion) | copy-start | bytes 49156
  20.2 10.6 %collective-permute-start.5 = (bf16[4,32,1024]{2,1,0:T(8,128)(2,1)S(1)}, bf16[4,32,1024]{2,1,0:T(8,128)(2,1)S(1)}, u32[]{:S(2)}, u32[]{:S(2)}) collective-permute-start(bf16[4,32,1024]{2,1,0:T(8,128)(2,1)S(1)} %collective-permute-done.4), channel_id=1, source_target_pairs={{0,1},{1,2},{2,3},{3,0},{4,5},{5,6},{6,7},{7,4},{8,9},{9,10},{10,1... | collective-permute-start | bytes 786440 | tf_op jit(solution)/shard_map/ppermute | solution.py:177
  31.9 1.9 copy-start.11
  33.8 23.5 %copy-start.2 = (bf16[4,4,32,1024]{3,2,1,0:T(8,128)(2,1)}, bf16[4,4,32,1024]{3,2,1,0:T(8,128)(2,1)S(1)}, u32[]{:S(2)}) copy-start(bf16[4,4,32,1024]{3,2,1,0:T(8,128)(2,1)S(1)} %gather_fusion) | copy-start | bytes 3145732
  35.0 22.4 %collective-permute-start.7 = (bf16[4,32,256]{2,1,0:T(8,128)(2,1)}, bf16[4,32,256]{2,1,0:T(8,128)(2,1)}, u32[]{:S(2)}, u32[]{:S(2)}) collective-permute-start(bf16[4,32,256]{2,1,0:T(8,128)(2,1)} %slice.88), channel_id=1, source_target_pairs={{0,496},{16,0},{32,16},{48,32},{64,48},{80,64},{96,80},{112,96},{1... | collective-permute-start | bytes 196616 | tf_op jit(solution)/shard_map/ppermute | solution.py:26
  53.0 13.1 %collective-permute-start = (bf16[4,32,1024]{2,1,0:T(8,128)(2,1)S(1)}, bf16[4,32,1024]{2,1,0:T(8,128)(2,1)S(1)}, u32[]{:S(2)}, u32[]{:S(2)}) collective-permute-start(bf16[4,32,1024]{2,1,0:T(8,128)(2,1)S(1)} %slice.79), channel_id=1, source_target_pairs={{0,496},{16,0},{32,16},{48,32},{64,48},{80,64},{96,80},{112,96},{1... | collective-permute-start | bytes 786440 | tf_op jit(solution)/shard_map/ppermute | solution.py:26
  57.3 8.7 %copy-start.8 = (bf16[16,32,1024]{2,1,0:T(8,128)(2,1)S(1)}, bf16[16,32,1024]{2,1,0:T(8,128)(2,1)}, u32[]{:S(2)}) copy-start(bf16[16,32,1024]{2,1,0:T(8,128)(2,1)} %all-gather.2.cloned.1.call-done) | copy-start | bytes 3145732
  58.8 29.4 %collective-permute-start.8 = (bf16[16,4,256]{2,1,0:T(4,128)(2,1)}, bf16[16,4,256]{2,1,0:T(4,128)(2,1)}, u32[]{:S(2)}, u32[]{:S(2)}) collective-permute-start(bf16[16,4,256]{2,1,0:T(4,128)(2,1)} %pad_maximum_fusion.6), channel_id=1, source_target_pairs={{0,12},{4,0},{8,4},{12,8},{1,13},{5,1},{9,5},{13,9},{2,14},{6,2},{... | collective-permute-start | bytes 98312 | tf_op jit(solution)/shard_map/ppermute | solution.py:26
  66.2 6.4 collective-permute-start.1
  77.3 1.0 copy-start.4
  85.7 5.4 copy-start.5
  85.8 8.1 %collective-permute-start.2 = (bf16[4,32,256]{2,1,0:T(8,128)(2,1)S(1)}, bf16[4,32,256]{2,1,0:T(8,128)(2,1)S(1)}, u32[]{:S(2)}, u32[]{:S(2)}) collective-permute-start(bf16[4,32,256]{2,1,0:T(8,128)(2,1)S(1)} %slice.85), channel_id=1, source_target_pairs={{0,16},{16,32},{32,48},{48,64},{64,80},{80,96},{96,112},{112,128},... | collective-permute-start | bytes 196616 | tf_op jit(solution)/shard_map/ppermute | solution.py:26
  93.9 10.2 %collective-permute-start.3 = (bf16[16,4,256]{2,1,0:T(4,128)(2,1)S(1)}, bf16[16,4,256]{2,1,0:T(4,128)(2,1)S(1)}, u32[]{:S(2)}, u32[]{:S(2)}) collective-permute-start(bf16[16,4,256]{2,1,0:T(4,128)(2,1)S(1)} %pad_maximum_fusion.7), channel_id=1, source_target_pairs={{0,4},{4,8},{8,12},{12,0},{1,5},{5,9},{9,13},{13,1},{2,6},{6,10},{... | collective-permute-start | bytes 98312 | tf_op jit(solution)/shard_map/ppermute | solution.py:26
  104.0 3.1 copy-start.14
  106.9 578.2 %reduce-scatter.6.cloned.1.call-start = ((), (), s32[]{:S(2)}) async-start(), calls=%async_computation.5 | async-start | bytes 1310720 | tf_op jit(solution)/shard_map/reduce_scatter | solution.py:96
  107.1 1.9 copy-start.3
  116.5 1.4 copy-start.7
  116.8 1.1 copy-start.6
  118.0 13.1 %collective-permute-start.9 = (bf16[4,32,3,256]{3,1,2,0:T(8,128)(2,1)S(1)}, bf16[4,32,3,256]{3,1,2,0:T(8,128)(2,1)S(1)}, u32[]{:S(2)}, u32[]{:S(2)}) collective-permute-start(bf16[4,32,3,256]{3,1,2,0:T(8,128)(2,1)S(1)} %slice.91), channel_id=1, source_target_pairs={{0,16},{16,32},{32,48},{48,64},{64,80},{80,96},{96,112},{112,128},... | collective-permute-start | bytes 589832 | tf_op jit(solution)/shard_map/ppermute | solution.py:26
  131.1 12.2 %copy-start.12 = (bf16[256,1024]{1,0:T(8,128)(2,1)S(1)}, bf16[256,1024]{1,0:T(8,128)(2,1)}, u32[]{:S(2)}) copy-start(bf16[256,1024]{1,0:T(8,128)(2,1)} %param.11) | copy-start | bytes 1572868
  131.1 10.0 %collective-permute-start.10 = (bf16[16,4,3,256]{3,1,2,0:T(4,128)(2,1)S(1)}, bf16[16,4,3,256]{3,1,2,0:T(4,128)(2,1)S(1)}, u32[]{:S(2)}, u32[]{:S(2)}) collective-permute-start(bf16[16,4,3,256]{3,1,2,0:T(4,128)(2,1)S(1)} %pad_maximum_fusion.5), channel_id=1, source_target_pairs={{0,4},{4,8},{8,12},{12,0},{1,5},{5,9},{9,13},{13,1},{2,6},{6,10},{... | collective-permute-start | bytes 294920 | tf_op jit(solution)/shard_map/ppermute | solution.py:26
  143.2 1.5 copy-start.13
  143.2 1.7 copy-start.21
  143.2 573.2 %reduce-scatter.4.cloned.1.call-start = ((), (), s32[]{:S(2)}) async-start(), calls=%async_computation.4 | async-start | bytes 1310720 | tf_op jit(solution)/shard_map/reduce_scatter | solution.py:96
  144.7 540.3 %copy-start.1 = (bf16[4,32,1024]{2,1,0:T(8,128)(2,1)S(1)}, bf16[4,32,1024]{2,1,0:T(8,128)(2,1)}, u32[]{:S(2)}) copy-start(bf16[4,32,1024]{2,1,0:T(8,128)(2,1)} %param.7) | copy-start | bytes 786436
  144.7 540.4 %copy-start.16 = (f32[4,32]{1,0:T(4,128)S(1)}, f32[4,32]{1,0:T(4,128)}, u32[]{:S(2)}) copy-start(f32[4,32]{1,0:T(4,128)} %copy-done.15) | copy-start | bytes 1540
  144.7 540.4 %copy-start.17 = (f32[1024]{0:T(1024)S(1)}, f32[1024]{0:T(1024)}, u32[]{:S(2)}) copy-start(f32[1024]{0:T(1024)} %param.9) | copy-start | bytes 12292
  144.7 540.4 %copy-start.19 = (f32[4,32]{1,0:T(4,128)S(1)}, f32[4,32]{1,0:T(4,128)}, u32[]{:S(2)}) copy-start(f32[4,32]{1,0:T(4,128)} %copy-done.18) | copy-start | bytes 1540
  144.7 571.7 %copy-start.10 = (bf16[4,32,1024]{2,1,0:T(8,128)(2,1)S(1)}, bf16[4,32,1024]{2,1,0:T(8,128)(2,1)}, u32[]{:S(2)}) copy-start(bf16[4,32,1024]{2,1,0:T(8,128)(2,1)} %param.13) | copy-start | bytes 786436
Sparse Core Ops, SparseCore 0:
  19.3 32.6 all-gather.1
  107.0 543.2 reduce-scatter.7
  653.4 31.6 reduce-scatter.5
  687.7 28.6 reduce-scatter.3
